TPU v7x, 32 devices: a whole 2x2x4 slice. The times are simulated.
32 devices in a mesh: gx: 4 (over y, x), gy: 8 (over z, core).
Axes of the slice: x: 2, y: 2, z: 4, core: 2. Of those that a mesh axis runs over, the one named last changes fastest.
Arguments:
- thermal_field: float32 [192, 192, 128], P('gx', 'gy'), may hold values from -6 to 6
- generator_keys: int32 [6], replicated, may hold values from 0 to 1048575
- slab_top_offset: int32 [1], replicated, may hold values from 0 to 2047
Outputs:
- factor_x: float32 [192, 64], P('gx')
- factor_y: float32 [192, 64], P('gy')
- factor_z: float32 [128, 64], replicated
- core: float32 [128, 128, 128], P('gx', 'gy')
All inputs are finite; a program needn't handle non-finite values.
Results may differ from a plain program's by a relative error of at most 0.000071.
Values sent between devices are 32-bit elements; how exact they have to be, the bound alone decides.
A program may use at most 64 MiB of HBM per device.

v0:
```python
import functools
import math

import jax
import jax.numpy as jnp
from jax import lax
from jax.experimental import pallas as pl
from jax.experimental.pallas import tpu as pltpu
from jax.sharding import PartitionSpec as P

RANK = 64
TARGET_RANK = 128


def random_signs(seed_value, cell_index, column_index):
    hashed = cell_index * 73856093 + column_index * 19349663 + seed_value * 83492791
    hashed = jnp.bitwise_xor(hashed, lax.shift_right_logical(hashed, jnp.full_like(hashed, 15)))
    hashed = hashed * 668265261
    hashed = jnp.bitwise_xor(hashed, lax.shift_right_logical(hashed, jnp.full_like(hashed, 13)))
    parity = jnp.bitwise_and(
        lax.shift_right_logical(hashed, jnp.full_like(hashed, 7)), jnp.full_like(hashed, 1)
    )
    return jnp.where(parity == 1, 1.0, -1.0).astype(jnp.float32)


def body(thermal_field, generator_keys, slab_top_offset):
    exact_matmul_mode = lax.Precision.HIGHEST
    front_length, back_length, vertical_layer = thermal_field.shape
    devices_first = lax.axis_size("gx")
    devices_second = lax.axis_size("gy")
    total_first = front_length * devices_first
    total_second = back_length * devices_second
    x_index = (lax.axis_index("gx") * front_length + jnp.arange(front_length, dtype=jnp.int32))[
        :, None
    ]
    y_index = (lax.axis_index("gy") * back_length + jnp.arange(back_length, dtype=jnp.int32))[
        :, None
    ]
    z_index = (slab_top_offset[0] + jnp.arange(vertical_layer, dtype=jnp.int32))[:, None]
    rank_cols = jnp.arange(RANK, dtype=jnp.int32)[None, :]
    core_cols = jnp.arange(TARGET_RANK, dtype=jnp.int32)[None, :]
    omega_x = random_signs(generator_keys[0], x_index, rank_cols)
    omega_y = random_signs(generator_keys[1], y_index, rank_cols)
    omega_z = random_signs(generator_keys[2], z_index, rank_cols)
    phi_xt = random_signs(generator_keys[3], x_index, core_cols).T
    phi_yt = random_signs(generator_keys[4], y_index, core_cols).T
    phi_z = random_signs(generator_keys[5], z_index, core_cols)
    unrolled_grid = thermal_field.reshape(front_length * back_length, vertical_layer)
    reduced = jnp.dot(unrolled_grid, omega_z, precision=exact_matmul_mode).reshape(
        front_length, back_length, RANK
    )
    partial_x = jnp.einsum("xyk,yk->xk", reduced, omega_y, precision=exact_matmul_mode)
    partial_y = jnp.einsum("xyk,xk->yk", reduced, omega_x, precision=exact_matmul_mode)
    khatri = (omega_x[:, None, :] * omega_y[None, :, :]).reshape(front_length * back_length, RANK)
    partial_z = jnp.einsum("pz,pk->zk", unrolled_grid, khatri, precision=exact_matmul_mode)
    summed_x, half_z = lax.psum((partial_x, partial_z), "gy")
    summed_y, summed_z = lax.psum((partial_y, half_z), "gx")
    factor_x = summed_x * (1.0 / math.sqrt(total_second * vertical_layer))
    factor_y = summed_y * (1.0 / math.sqrt(total_first * vertical_layer))
    factor_z = summed_z * (1.0 / math.sqrt(total_first * total_second))
    thermal_matrix = thermal_field.reshape(front_length, back_length * vertical_layer)
    chosen_entries = phi_xt
    reduced_first = lax.psum_scatter(
        jnp.dot(chosen_entries, thermal_matrix, precision=exact_matmul_mode),
        "gx",
        scatter_dimension=0,
        tiled=True,
    )
    reduced_first = reduced_first.reshape(-1, back_length, vertical_layer)
    chosen_entries = phi_yt
    middle = jnp.einsum("by,ayz->baz", chosen_entries, reduced_first, precision=exact_matmul_mode)
    swapped = lax.psum_scatter(
        jnp.einsum("baz,zc->bac", middle, phi_z, precision=exact_matmul_mode),
        "gy",
        scatter_dimension=0,
        tiled=True,
    )
    core_block = jnp.transpose(swapped, (1, 0, 2))
    core = core_block * (1.0 / math.sqrt(total_first * total_second * vertical_layer))
    return (factor_x, factor_y, factor_z, core)


SUB = 8
LANES = 128
MESH_ID = pl.DeviceIdType.MESH


def signs(seed_value, cell_index, column_index):
    hashed = cell_index * 73856093 + column_index * 19349663 + seed_value * 83492791
    hashed = hashed ^ lax.shift_right_logical(hashed, jnp.full_like(hashed, 15))
    hashed = hashed * 668265261
    hashed = hashed ^ lax.shift_right_logical(hashed, jnp.full_like(hashed, 13))
    return jnp.where((hashed & 128) != 0, 1.0, -1.0).astype(jnp.float32)


def iota(shape, axis):
    return lax.broadcasted_iota(jnp.int32, shape, axis)


def split(value):
    high = value.astype(jnp.bfloat16)
    low = (value - high.astype(jnp.float32)).astype(jnp.bfloat16)
    return high, low


def mm(left, right):
    return jnp.dot(left, right, preferred_element_type=jnp.float32)


def flip(index, bit):
    return index + bit - 2 * bit * ((index // bit) % 2)


def way_of(group, groups, core):
    if 2 * group + 1 == groups:
        return core
    return 0 if 2 * group < groups else 1


def step_x(ix, way, turn):
    low = flip(ix, 1)
    high = flip(ix, 2)
    first = low + (high - low) * way
    return first if turn == 0 else low + high - first


def kernel(
    dims,
    keys, top, field_in,
    out_x, out_y, out_z, out_core,
    field, load_sem, raw_out, raw_in, spread, landed, own, near, far_out, far_in, done_out, done_in, kron,
    small_out, small_in, small_sum, zsum_in, zx_out, zx_in, fy_out, fy_in,
    s0, r0, s5, r5, s1, r1, s2, r2, s3, r3, s4, r4, t1, u1, t2, u2, t3, u3, t4, u4,
):
    nx, ng, front, back, depth = dims
    nz = ng // 2
    blk_a = TARGET_RANK // nx
    chunks = blk_a // (2 * SUB)
    blk_b = TARGET_RANK // nz
    out_b = blk_b // 2
    ix = lax.axis_index("gx")
    ig = lax.axis_index("gy")
    iz, core = ig // 2, ig % 2

    def dev_x(d):
        r = ix
        for bit in (1, 2):
            if d & bit:
                r = flip(r, bit)
        return r

    def dev_g(d):
        r = ig
        for bit in (1, 2, 4):
            if d & bit:
                r = flip(r, bit)
        return r

    def copy(src, dst, send, recv, dx, dg):
        return pltpu.make_async_remote_copy(
            src_ref=src, dst_ref=dst, send_sem=send, recv_sem=recv,
            device_id=(dev_x(dx), dev_g(dg)), device_id_type=MESH_ID,
        )

    partners = [(dx, dc) for dx in range(nx) for dc in range(2) if dx or dc]
    partners += [(0, dg) for dg in range(2, ng)]
    barrier = pltpu.get_barrier_semaphore()
    for dx, dg in partners:
        pl.semaphore_signal(
            barrier, inc=1, device_id=(dev_x(dx), dev_g(dg)), device_id_type=MESH_ID
        )

    x0 = ix * front
    y0 = ig * back
    z0 = top[0]

    groups = back // SUB
    fold = front // 2
    deep = depth // 2
    load = pltpu.make_async_copy(field_in, field, load_sem)
    load.start()
    two_d = field.reshape(front * back, depth)
    x0 = ix * front
    y0 = ig * back
    z0 = top[0]
    lower = iota((fold, SUB, depth), 2) < deep
    raws = []
    load.wait()
    for h in range(2):
        for g in range(groups):
            here = field[0:fold, g * SUB : (g + 1) * SUB, :]
            there = field[fold:front, g * SUB : (g + 1) * SUB, :]
            if h == 0:
                raw_out[h, g] = jnp.where(lower, here, pltpu.roll(there, deep, 2))
            else:
                raw_out[h, g] = jnp.where(lower, pltpu.roll(here, deep, 2), there)
    pl.semaphore_wait(barrier, len(partners))
    for h in range(2):
        for g in range(groups):
            near_x = step_x(ix, way_of(g, groups, core), 0)
            raws.append(pltpu.make_async_remote_copy(
                src_ref=raw_out.at[h, g], dst_ref=raw_in.at[h, g],
                send_sem=s0.at[h, g], recv_sem=r0.at[h, g],
                device_id=(near_x, ig), device_id_type=MESH_ID,
            ))
            raws[-1].start()
    pend = list(raws)

    pairs = blk_a // 2

    def weights(base, far_x):
        shape = (4 * pairs, 4 * fold)
        row = iota(shape, 0)
        lane = iota(shape, 1)
        lane = jnp.where(lane >= front, lane - front, lane)
        second = row >= 2 * pairs
        row = jnp.where(second, row - 2 * pairs, row)
        swapped = jnp.where(lane >= fold, lane - fold, lane + fold)
        cell = jnp.where(second, swapped, lane) + base
        target = jnp.where(row < pairs, ix * blk_a, far_x * blk_a - pairs) + row
        target = jnp.where(second, target + pairs, target)
        return signs(keys[3], cell, target).astype(jnp.bfloat16)

    lower_row = iota((2 * pairs, depth), 1) < deep

    def contract(left, packed):
        both = jnp.concatenate([packed, pltpu.roll(packed, deep, 1)], axis=0)
        high, low = split(both)
        out = mm(left, jnp.concatenate([high, low], axis=0))
        return jnp.where(lower_row, out[: 2 * pairs], out[2 * pairs :])

    for g in range(groups):
        way = way_of(g, groups, core)
        left = weights(x0, step_x(ix, way, 1))
        for h in range(2):
            flat = raw_out.at[h, g].reshape(fold * SUB, depth)
            for y in range(SUB):
                spread[h, g * SUB + y] = contract(left, flat[pl.ds(y, fold, stride=SUB), :])
    lane = iota((RANK, 2 * front), 1)
    left = signs(
        keys[0], jnp.where(lane >= front, lane - front, lane) + x0, iota((RANK, 2 * front), 0)
    ).astype(jnp.bfloat16)
    omega_yt = signs(keys[1], iota((RANK, back), 1) + y0, iota((RANK, back), 0))
    total_z = jnp.zeros((RANK, depth), jnp.float32)
    for y in range(back):
        high, low = split(two_d[pl.ds(y, front, stride=back), :])
        both = mm(left, jnp.concatenate([high, low], axis=0))
        total_z = total_z + both * omega_yt[:, y : y + 1]

    lane_z = iota((depth, LANES), 1)
    row_z = iota((depth, LANES), 0) + z0
    omega_z = signs(keys[2], row_z, lane_z).astype(jnp.bfloat16)
    high, low = split(two_d[...])
    reduced = (mm(high, omega_z) + mm(low, omega_z)).reshape(front, back, LANES)
    omega_y = signs(keys[1], iota((back, LANES), 0) + y0, iota((back, LANES), 1))
    part_y = jnp.zeros((back, LANES), jnp.float32)
    omega_x = signs(keys[0], iota((front, LANES), 0) + x0, iota((front, LANES), 1))
    part_x = jnp.sum(reduced * omega_y[None], axis=1)
    for x in range(front):
        part_y = part_y + reduced[x] * omega_x[x : x + 1]
    fy_out[...] = part_y
    per = front // ng
    kper = RANK // ng
    for d in range(ng):
        small_out[d, 0:kper] = total_z[d * kper : (d + 1) * kper]
        small_out[d, SUB : SUB + per] = part_x[d * per : (d + 1) * per]
    fy = []
    for d in range(1, nx):
        fy.append(copy(fy_out, fy_in.at[d - 1], t1.at[d - 1], u1.at[d - 1], d, 0))
        fy[-1].start()
    sm = []
    for d in range(1, ng):
        sm.append(copy(
            small_out.at[dev_g(d)], small_in.at[d - 1], t2.at[d - 1], u2.at[d - 1], 0, d
        ))
        sm[-1].start()
    pend += fy

    half = 2 * back * SUB
    for dst in range(2):
        for src in range(2):
            for dc in range(2):
                shape = (blk_b * SUB, back * SUB)
                row = iota(shape, 0)
                col = iota(shape, 1)
                chip_b = (flip(iz, 2) if dst else iz) * blk_b
                cell_y = dev_g(src * 2 + dc) * back
                value = signs(
                    keys[4],
                    lax.shift_right_logical(col, jnp.full_like(col, 3)) + cell_y,
                    lax.shift_right_logical(row, jnp.full_like(row, 3)) + chip_b,
                )
                value = jnp.where((row & 7) == (col & 7), value, 0.0)
                kron[src, dc, dst * blk_b * SUB : (dst + 1) * blk_b * SUB, :] = value.astype(
                    jnp.bfloat16
                )
    row = iota((depth, 2 * LANES), 0)
    col = iota((depth, 2 * LANES), 1)
    same = (row >= deep) == (col >= LANES)
    row = jnp.where(row >= deep, row - deep, row) + z0
    col = jnp.where(col >= LANES, col - LANES, col)
    phi_z = [
        jnp.where(same, signs(keys[5], row + h * deep, col), 0.0).astype(jnp.bfloat16)
        for h in range(2)
    ]

    def project(src, dc, block):
        high, low = split(block.reshape(back * SUB, depth))
        return mm(kron[src, dc], high) + mm(kron[src, dc], low)

    sends = [[] for _ in range(chunks)]
    lefts = []
    for g in range(groups):
        way = way_of(g, groups, core)
        lefts.append(weights(step_x(ix, way, 0) * front, step_x(ix, way, 1)))
    for i in range(chunks):
        for g in range(groups):
            raws[i * groups + g].wait_recv()
            flat = raw_in.at[i, g].reshape(fold * SUB, depth)
            for y in range(SUB):
                spread[i, g * SUB + y] += contract(
                    lefts[g], flat[pl.ds(y, fold, stride=SUB), :]
                )
            for dc in (1, 0):
                start = pl.multiple_of(pairs + (dev_g(dc) % 2) * SUB, SUB)
                sends[i].append(pltpu.make_async_remote_copy(
                    src_ref=spread.at[i, g * SUB : (g + 1) * SUB, pl.ds(start, SUB), :],
                    dst_ref=landed.at[i, dc, g * SUB : (g + 1) * SUB],
                    send_sem=s1.at[i, dc, g], recv_sem=r1.at[i, dc, g],
                    device_id=(step_x(ix, way_of(g, groups, core), 1), dev_g(dc)),
                    device_id_type=MESH_ID,
                ))
                sends[i][-1].start()
        start = pl.multiple_of((1 - core) * SUB, SUB)
        sends[i].append(copy(
            spread.at[i, :, pl.ds(start, SUB), :], landed.at[i, 2], s5.at[i], r5.at[i], 0, 1
        ))
        sends[i][-1].start()
    pend += sum(sends, [])

    nearby = []
    sums = []
    for i in range(chunks):
        for c in sends[i]:
            c.wait_recv()
        own[i, 0] = spread[i, :, pl.ds(pl.multiple_of(core * SUB, SUB), SUB), :] + landed[i, 0]
        own[i, 1] = landed[i, 2] + landed[i, 1]
        c = copy(own.at[i], near.at[i], s2.at[i], r2.at[i], 0, 2)
        c.start()
        nearby.append(c)
        sums.append(project(0, 0, own[i, 0]) + project(0, 1, own[i, 1]))
    pend += nearby

    for c in sm:
        c.wait_recv()
    block = small_out[ig]
    for d in range(1, ng):
        block = block + small_in[d - 1]
    small_sum[...] = block
    zx = []
    for d in range(1, nx):
        zx.append(copy(
            small_sum.at[0:SUB], zsum_in.at[d - 1], t3.at[d - 1], u3.at[d - 1], d, 0
        ))
        zx[-1].start()
    pend += zx

    far = []
    for i in range(chunks):
        nearby[i].wait_recv()
        total = sums[i] + project(1, 0, near[i, 0]) + project(1, 1, near[i, 1])
        far_out[i] = total[blk_b * SUB :]
        c = copy(far_out.at[i], far_in.at[i], s3.at[i], r3.at[i], 0, 4)
        c.start()
        far.append(c)
        sums[i] = total[: blk_b * SUB]
    pend += far

    for c in zx:
        c.wait_recv()
    zpart = small_sum[0:SUB]
    for d in range(1, nx):
        zpart = zpart + zsum_in[d - 1]
    zx_out[0:SUB] = zpart
    zx_out[SUB:] = small_sum[SUB:]
    gathered = []
    for d in range(1, ng):
        gathered.append(copy(zx_out, zx_in.at[d - 1], t4.at[d - 1], u4.at[d - 1], 0, d))
        gathered[-1].start()
    pend += gathered
    for c in fy:
        c.wait_recv()
    value = fy_out[...]
    for d in range(1, nx):
        value = value + fy_in[d - 1]
    out_y[...] = (value * (1.0 / math.sqrt(front * nx * depth)))[:, :RANK]

    scale = 1.0 / math.sqrt(front * nx * back * ng * depth)
    finals = []
    mine = 0.0

    def last(i, block):
        high, low = split(block)
        return mm(high, phi_z[i]) + mm(low, phi_z[i])

    def put(which, value):
        value = value * scale
        for i in range(chunks):
            for b in range(out_b):
                out_core[pl.ds((i * pairs + which * SUB) * out_b + b, SUB, stride=out_b), :] = (
                    value[b * SUB : (b + 1) * SUB, i * LANES : (i + 1) * LANES]
                )

    for i in range(chunks):
        far[i].wait_recv()
        done_out[i] = (sums[i] + far_in[i]).reshape(2, out_b * SUB, depth)
        c = copy(done_out.at[i, 1 - core], done_in.at[i], s4.at[i], r4.at[i], 0, 1)
        c.start()
        finals.append(c)
        mine = mine + last(i, done_out[i, core])
    put(core, mine)
    pend += finals

    for c in gathered:
        c.wait_recv()
    for c in sm:
        c.wait_send()
    for d in range(ng):
        block = zx_out[...] if d == 0 else zx_in[d - 1]
        small_out[dev_g(d)] = block
    scale_x = 1.0 / math.sqrt(back * ng * depth)
    scale_z = 1.0 / math.sqrt(front * nx * back * ng)
    for d in range(ng):
        out_x[d * per : (d + 1) * per, :] = small_out[d, SUB : SUB + per, :RANK] * scale_x
    whole = jnp.concatenate([small_out[d, 0:kper] for d in range(ng)], axis=0)
    out_z[...] = whole.T * scale_z

    other = 0.0
    for i in range(chunks):
        finals[i].wait_recv()
        other = other + last(i, done_in[i])
    put(1 - core, other)
    for c in pend:
        c.wait_send()


def fused_body(nx, ng, thermal_field, generator_keys, slab_top_offset):
    front, back, depth = thermal_field.shape
    nz = ng // 2
    blk_a = TARGET_RANK // nx
    chunks = blk_a // (2 * SUB)
    blk_b = TARGET_RANK // nz
    out_b = blk_b // 2
    f32 = jnp.float32
    vmem = pltpu.VMEM
    dma = pltpu.SemaphoreType.DMA
    groups = back // SUB
    scratch = [
        vmem((front, back, depth), f32),
        dma(()),
        vmem((2, groups, front // 2, SUB, depth), f32),
        vmem((2, groups, front // 2, SUB, depth), f32),
        vmem((2, back, blk_a, depth), f32),
        vmem((chunks, 3, back, SUB, depth), f32),
        vmem((chunks, 2, back, SUB, depth), f32),
        vmem((chunks, 2, back, SUB, depth), f32),
        vmem((chunks, blk_b * SUB, depth), f32),
        vmem((chunks, blk_b * SUB, depth), f32),
        vmem((chunks, 2, out_b * SUB, depth), f32),
        vmem((chunks, out_b * SUB, depth), f32),
        vmem((2, 2, 2 * blk_b * SUB, back * SUB), jnp.bfloat16),
        vmem((ng, 2 * SUB, LANES), f32),
        vmem((ng - 1, 2 * SUB, LANES), f32),
        vmem((2 * SUB, LANES), f32),
        vmem((nx - 1, SUB, LANES), f32),
        vmem((2 * SUB, LANES), f32),
        vmem((ng - 1, 2 * SUB, LANES), f32),
        vmem((back, LANES), f32),
        vmem((nx - 1, back, LANES), f32),
        dma((2, groups)), dma((2, groups)),
        dma((chunks,)), dma((chunks,)),
        dma((chunks, 2, groups)), dma((chunks, 2, groups)),
        dma((chunks,)), dma((chunks,)),
        dma((chunks,)), dma((chunks,)),
        dma((chunks,)), dma((chunks,)),
        dma((nx - 1,)), dma((nx - 1,)),
        dma((ng - 1,)), dma((ng - 1,)),
        dma((nx - 1,)), dma((nx - 1,)),
        dma((ng - 1,)), dma((ng - 1,)),
    ]
    whole = pl.BlockSpec(memory_space=pltpu.VMEM)
    scalar = pl.BlockSpec(memory_space=pltpu.SMEM)
    fx, fy, fz, core = pl.pallas_call(
        functools.partial(kernel, (nx, ng, front, back, depth)),
        out_shape=(
            jax.ShapeDtypeStruct((front, RANK), f32),
            jax.ShapeDtypeStruct((back, RANK), f32),
            jax.ShapeDtypeStruct((depth, RANK), f32),
            jax.ShapeDtypeStruct((blk_a * out_b, depth), f32),
        ),
        in_specs=[scalar, scalar, pl.BlockSpec(memory_space=pl.ANY)],
        out_specs=(whole,) * 4,
        scratch_shapes=scratch,
        compiler_params=pltpu.CompilerParams(
            collective_id=0, has_side_effects=True, vmem_limit_bytes=40 * 2**20
        ),
    )(generator_keys, slab_top_offset, thermal_field)
    return fx, fy, fz, core.reshape(blk_a, out_b, depth)


def suits(nx, ng):
    return nx == 4 and ng == 8


def solution(mesh):
    nx, ng = mesh.shape["gx"], mesh.shape["gy"]
    chosen = functools.partial(fused_body, nx, ng) if suits(nx, ng) else body
    placed = (P("gx", "gy", None), P(), P())
    return jax.shard_map(
        chosen,
        mesh=mesh,
        in_specs=placed,
        out_specs=(P("gx", None), P("gy", None), P(), P("gx", "gy", None)),
        check_vma=False,
    )
```

profile of v0, /device:TPU:0, one launch (start us, length us, event | category | flops | bytes accessed | tf_op | source)
XLA Modules:
  0.0 45.7 jit_solution(14077026156877280327)
XLA Ops:
  0.6 0.0 copy-start.1
  1.3 0.0 copy-done.1
  1.3 0.0 copy-start
  1.3 1.1 %copy-done = f32[48,24,128]{2,1,0:T(8,128)S(1)} copy-done((f32[48,24,128]{2,1,0:T(8,128)S(1)}, f32[48,24,128]{2,1,0:T(8,128)}, u32[]{:S(2)}) %copy-start) | copy-done | bytes 589848
  2.4 40.7 %shard_map.66 = (f32[48,64]{1,0:T(8,128)S(1)}, f32[24,64]{1,0:T(8,128)S(1)}, f32[128,64]{1,0:T(8,128)S(1)}, f32[512,128]{1,0:T(8,128)S(1)}) custom-call(s32[6]{0:T(128)S(1)} %copy-done.1, s32[1]{0:T(128)S(6)} %copy.11.top, f32[48,24,128]{2,1,0:T(8,128)S(1)} %copy-done), custom_call_target="tpu_custom_call" | custom-call | tf_op jit(solution)/shard_map/pallas_call | solution.py:493
  43.1 0.7 %copy.7 = f32[128,64]{0,1:T(8,128)} copy(f32[128,64]{1,0:T(8,128)S(1)} %get-tuple-element.14) | data formatting | bytes 65536
  43.8 0.6 %copy.12 = f32[48,64]{1,0:T(8,128)} copy(f32[48,64]{1,0:T(8,128)S(1)} %get-tuple-element.20) | data formatting | bytes 24576
  44.4 0.6 %copy.13 = f32[24,64]{1,0:T(8,128)} copy(f32[24,64]{1,0:T(8,128)S(1)} %get-tuple-element.21) | data formatting | bytes 12288
  45.0 0.7 %copy.14 = f32[32,16,128]{2,1,0:T(8,128)} copy(f32[32,16,128]{2,1,0:T(8,128)S(1)} %bitcast.1) | data formatting | bytes 524288
Async XLA Ops:
  0.6 0.7 %copy-start.1 = (s32[6]{0:T(128)S(1)}, s32[6]{0:T(128)}, u32[]{:S(2)}) copy-start(s32[6]{0:T(128)} %keys.1) | copy-start | bytes 76
  1.3 1.1 %copy-start = (f32[48,24,128]{2,1,0:T(8,128)S(1)}, f32[48,24,128]{2,1,0:T(8,128)}, u32[]{:S(2)}) copy-start(f32[48,24,128]{2,1,0:T(8,128)} %field_in.1) | copy-start | bytes 1769476
where the time goes:
time: 46 us; the launch traced here: 45.7 us
  Pallas kernels  40.7 us (88%)
  local copies, waits for them, and re-layouts  3.67 us (8%)
  between operations  1.32 us (3%)
    pallas_call x1, Pallas kernels, fused_body(): pl.pallas_call(functools.partial(kernel, (nx, ng, front, back, depth)), o...  40.7 us
    unnamed x8, local copies, waits for them, and re-layouts  3.67 us

commit v1 on v0

v1 whole, which is shorter than its diff:
```python
import functools
import math

import jax
import jax.numpy as jnp
from jax import lax
from jax.experimental import pallas as pl
from jax.experimental.pallas import tpu as pltpu
from jax.sharding import PartitionSpec as P

RANK = 64
TARGET_RANK = 128


def random_signs(seed_value, cell_index, column_index):
    hashed = cell_index * 73856093 + column_index * 19349663 + seed_value * 83492791
    hashed = jnp.bitwise_xor(hashed, lax.shift_right_logical(hashed, jnp.full_like(hashed, 15)))
    hashed = hashed * 668265261
    hashed = jnp.bitwise_xor(hashed, lax.shift_right_logical(hashed, jnp.full_like(hashed, 13)))
    parity = jnp.bitwise_and(
        lax.shift_right_logical(hashed, jnp.full_like(hashed, 7)), jnp.full_like(hashed, 1)
    )
    return jnp.where(parity == 1, 1.0, -1.0).astype(jnp.float32)


def body(thermal_field, generator_keys, slab_top_offset):
    exact_matmul_mode = lax.Precision.HIGHEST
    front_length, back_length, vertical_layer = thermal_field.shape
    devices_first = lax.axis_size("gx")
    devices_second = lax.axis_size("gy")
    total_first = front_length * devices_first
    total_second = back_length * devices_second
    x_index = (lax.axis_index("gx") * front_length + jnp.arange(front_length, dtype=jnp.int32))[
        :, None
    ]
    y_index = (lax.axis_index("gy") * back_length + jnp.arange(back_length, dtype=jnp.int32))[
        :, None
    ]
    z_index = (slab_top_offset[0] + jnp.arange(vertical_layer, dtype=jnp.int32))[:, None]
    rank_cols = jnp.arange(RANK, dtype=jnp.int32)[None, :]
    core_cols = jnp.arange(TARGET_RANK, dtype=jnp.int32)[None, :]
    omega_x = random_signs(generator_keys[0], x_index, rank_cols)
    omega_y = random_signs(generator_keys[1], y_index, rank_cols)
    omega_z = random_signs(generator_keys[2], z_index, rank_cols)
    phi_xt = random_signs(generator_keys[3], x_index, core_cols).T
    phi_yt = random_signs(generator_keys[4], y_index, core_cols).T
    phi_z = random_signs(generator_keys[5], z_index, core_cols)
    unrolled_grid = thermal_field.reshape(front_length * back_length, vertical_layer)
    reduced = jnp.dot(unrolled_grid, omega_z, precision=exact_matmul_mode).reshape(
        front_length, back_length, RANK
    )
    partial_x = jnp.einsum("xyk,yk->xk", reduced, omega_y, precision=exact_matmul_mode)
    partial_y = jnp.einsum("xyk,xk->yk", reduced, omega_x, precision=exact_matmul_mode)
    khatri = (omega_x[:, None, :] * omega_y[None, :, :]).reshape(front_length * back_length, RANK)
    partial_z = jnp.einsum("pz,pk->zk", unrolled_grid, khatri, precision=exact_matmul_mode)
    summed_x, half_z = lax.psum((partial_x, partial_z), "gy")
    summed_y, summed_z = lax.psum((partial_y, half_z), "gx")
    factor_x = summed_x * (1.0 / math.sqrt(total_second * vertical_layer))
    factor_y = summed_y * (1.0 / math.sqrt(total_first * vertical_layer))
    factor_z = summed_z * (1.0 / math.sqrt(total_first * total_second))
    thermal_matrix = thermal_field.reshape(front_length, back_length * vertical_layer)
    chosen_entries = phi_xt
    reduced_first = lax.psum_scatter(
        jnp.dot(chosen_entries, thermal_matrix, precision=exact_matmul_mode),
        "gx",
        scatter_dimension=0,
        tiled=True,
    )
    reduced_first = reduced_first.reshape(-1, back_length, vertical_layer)
    chosen_entries = phi_yt
    middle = jnp.einsum("by,ayz->baz", chosen_entries, reduced_first, precision=exact_matmul_mode)
    swapped = lax.psum_scatter(
        jnp.einsum("baz,zc->bac", middle, phi_z, precision=exact_matmul_mode),
        "gy",
        scatter_dimension=0,
        tiled=True,
    )
    core_block = jnp.transpose(swapped, (1, 0, 2))
    core = core_block * (1.0 / math.sqrt(total_first * total_second * vertical_layer))
    return (factor_x, factor_y, factor_z, core)


SUB = 8
LANES = 128
PARTS = 2
MESH_ID = pl.DeviceIdType.MESH


def signs(seed_value, cell_index, column_index):
    hashed = cell_index * 73856093 + column_index * 19349663 + seed_value * 83492791
    hashed = hashed ^ lax.shift_right_logical(hashed, jnp.full_like(hashed, 15))
    hashed = hashed * 668265261
    hashed = hashed ^ lax.shift_right_logical(hashed, jnp.full_like(hashed, 13))
    return jnp.where((hashed & 128) != 0, 1.0, -1.0).astype(jnp.float32)


def iota(shape, axis):
    return lax.broadcasted_iota(jnp.int32, shape, axis)


def split(value):
    high = value.astype(jnp.bfloat16)
    low = (value - high.astype(jnp.float32)).astype(jnp.bfloat16)
    return high, low


def mm(left, right):
    return jnp.dot(left, right, preferred_element_type=jnp.float32)


def flip(index, bit):
    return index + bit - 2 * bit * ((index // bit) % 2)


def way_of(group, groups, core):
    if 2 * group + 1 == groups:
        return core
    return 0 if 2 * group < groups else 1


def step_x(ix, way, turn):
    low = flip(ix, 1)
    high = flip(ix, 2)
    first = low + (high - low) * way
    return first if turn == 0 else low + high - first


def kernel(
    dims,
    keys_in, top, field_in,
    out_x, out_y, out_z, out_core,
    keys, field, load_sem, raw_out, raw_in, spread, landed, own, near, keep, part_out, part_in,
    first_w, second_w, phi_y, phi_z,
    small_out, small_in, small_sum, zsum_in, zx_out, zx_in, fy_out, fy_in,
    s0, r0, s5, r5, s1, r1, s2, r2, s3, r3, t1, u1, t2, u2, t3, u3, t4, u4,
):
    nx, ng, front, back, depth = dims
    nz = ng // 2
    blk_a = TARGET_RANK // nx
    pairs = blk_a // 2
    out_b = TARGET_RANK // ng
    ix = lax.axis_index("gx")
    ig = lax.axis_index("gy")
    iz, core = ig // 2, ig % 2

    def dev_x(d):
        r = ix
        for bit in (1, 2):
            if d & bit:
                r = flip(r, bit)
        return r

    def dev_g(d):
        r = ig
        for bit in (1, 2, 4):
            if d & bit:
                r = flip(r, bit)
        return r

    def copy(src, dst, send, recv, dx, dg):
        return pltpu.make_async_remote_copy(
            src_ref=src, dst_ref=dst, send_sem=send, recv_sem=recv,
            device_id=(dev_x(dx), dev_g(dg)), device_id_type=MESH_ID,
        )

    load = pltpu.make_async_copy(field_in, field, load_sem.at[0])
    load.start()
    load_keys = pltpu.make_async_copy(keys_in, keys, load_sem.at[1])
    load_keys.start()
    partners = [(dx, dc) for dx in range(nx) for dc in range(2) if dx or dc]
    partners += [(0, dg) for dg in range(2, ng)]
    barrier = pltpu.get_barrier_semaphore()
    for dx, dg in partners:
        pl.semaphore_signal(
            barrier, inc=1, device_id=(dev_x(dx), dev_g(dg)), device_id_type=MESH_ID
        )

    x0 = ix * front
    y0 = ig * back
    groups = back // SUB
    order = list(range(0, groups, 2)) + list(range(1, groups, 2))
    fold = front // 2
    deep = depth // 2
    two_d = field.reshape(front * back, depth)
    lower = iota((fold, SUB, depth), 2) < deep
    load.wait()
    for h in range(2):
        for g in range(groups):
            here = field[0:fold, g * SUB : (g + 1) * SUB, :]
            there = field[fold:front, g * SUB : (g + 1) * SUB, :]
            if h == 0:
                raw_out[h, g] = jnp.where(lower, here, pltpu.roll(there, deep, 2))
            else:
                raw_out[h, g] = jnp.where(lower, pltpu.roll(here, deep, 2), there)
    pl.semaphore_wait(barrier, len(partners))
    raws = {}
    for h in range(2):
        for g in order:
            raws[h, g] = pltpu.make_async_remote_copy(
                src_ref=raw_out.at[h, g], dst_ref=raw_in.at[h, g],
                send_sem=s0.at[h, g], recv_sem=r0.at[h, g],
                device_id=(step_x(ix, way_of(g, groups, core), 0), ig), device_id_type=MESH_ID,
            )
            raws[h, g].start()
    pend = list(raws.values())
    load_keys.wait()
    z0 = top[0]

    lane = iota((RANK, 2 * front), 1)
    left = signs(
        keys[0], jnp.where(lane >= front, lane - front, lane) + x0, iota((RANK, 2 * front), 0)
    ).astype(jnp.bfloat16)
    omega_yt = signs(keys[1], iota((RANK, back), 1) + y0, iota((RANK, back), 0))
    total_z = jnp.zeros((RANK, depth), jnp.float32)
    for y in range(back):
        high, low = split(two_d[pl.ds(y, front, stride=back), :])
        both = mm(left, jnp.concatenate([high, low], axis=0))
        total_z = total_z + both * omega_yt[:, y : y + 1]

    lane_z = iota((depth, LANES), 1)
    row_z = iota((depth, LANES), 0) + z0
    omega_z = signs(keys[2], row_z, lane_z).astype(jnp.bfloat16)
    high, low = split(two_d[...])
    reduced = (mm(high, omega_z) + mm(low, omega_z)).reshape(front, back, LANES)
    omega_y = signs(keys[1], iota((back, LANES), 0) + y0, iota((back, LANES), 1))
    part_y = jnp.zeros((back, LANES), jnp.float32)
    omega_x = signs(keys[0], iota((front, LANES), 0) + x0, iota((front, LANES), 1))
    part_x = jnp.sum(reduced * omega_y[None], axis=1)
    for x in range(front):
        part_y = part_y + reduced[x] * omega_x[x : x + 1]
    fy_out[...] = part_y
    per = front // ng
    kper = RANK // ng
    for d in range(ng):
        small_out[d, 0:kper] = total_z[d * kper : (d + 1) * kper]
        small_out[d, SUB : SUB + per] = part_x[d * per : (d + 1) * per]
    fy = []
    for d in range(1, nx):
        fy.append(copy(fy_out, fy_in.at[d - 1], t1.at[d - 1], u1.at[d - 1], d, 0))
        fy[-1].start()
    sm = []
    for d in range(1, ng):
        sm.append(copy(
            small_out.at[dev_g(d)], small_in.at[d - 1], t2.at[d - 1], u2.at[d - 1], 0, d
        ))
        sm[-1].start()
    pend += fy

    def weights(base, far_x):
        shape = (4 * pairs, 4 * fold)
        row = iota(shape, 0)
        lane = iota(shape, 1)
        lane = jnp.where(lane >= front, lane - front, lane)
        second = row >= 2 * pairs
        row = jnp.where(second, row - 2 * pairs, row)
        swapped = jnp.where(lane >= fold, lane - fold, lane + fold)
        cell = jnp.where(second, swapped, lane) + base
        target = jnp.where(row < pairs, ix * blk_a, far_x * blk_a - pairs) + row
        target = jnp.where(second, target + pairs, target)
        return signs(keys[3], cell, target).astype(jnp.bfloat16)

    for g in range(groups):
        way = way_of(g, groups, core)
        first_w[g] = weights(x0, step_x(ix, way, 1))
        second_w[g] = weights(step_x(ix, way, 0) * front, step_x(ix, way, 1))

    lower_row = iota((2 * pairs, depth), 1) < deep

    def contract(left, packed):
        both = jnp.concatenate([packed, pltpu.roll(packed, deep, 1)], axis=0)
        high, low = split(both)
        out = mm(left, jnp.concatenate([high, low], axis=0))
        return jnp.where(lower_row, out[: 2 * pairs], out[2 * pairs :])

    for h in range(2):
        wide = spread.at[h].reshape(2 * pairs * back, depth)
        for g in order:
            flat = raw_out.at[h, g].reshape(fold * SUB, depth)
            for y in range(SUB):
                wide[pl.ds(g * SUB + y, 2 * pairs, stride=back), :] = contract(
                    first_w[g], flat[pl.ds(y, fold, stride=SUB), :]
                )

    shape = (4 * out_b, 4 * back)
    row = iota(shape, 0)
    col = iota(shape, 1)
    col = jnp.where(col >= 2 * back, col - 2 * back, col)
    target = row
    for k, d in enumerate((0, 1, 4, 5)):
        target = jnp.where(row >= k * out_b, row + (dev_g(d) - k) * out_b, target)
    for src in range(2):
        cell = jnp.where(col >= back, dev_g(2 * src + 1) * back - back, dev_g(2 * src) * back) + col
        phi_y[:, src * 4 * back : (src + 1) * 4 * back] = signs(keys[4], cell, target).astype(
            jnp.bfloat16
        )
    row = iota((depth, 2 * LANES), 0)
    col = iota((depth, 2 * LANES), 1)
    same = (row >= deep) == (col >= LANES)
    row = jnp.where(row >= deep, row - deep, row) + z0
    col = jnp.where(col >= LANES, col - LANES, col)
    for h in range(2):
        phi_z[h] = jnp.where(same, signs(keys[5], row + h * deep, col), 0.0).astype(jnp.bfloat16)

    def receive_raw(h):
        wide = spread.at[h].reshape(2 * pairs * back, depth)
        sends = []
        for g in order:
            raws[h, g].wait_recv()
            flat = raw_in.at[h, g].reshape(fold * SUB, depth)
            for y in range(SUB):
                place = pl.ds(g * SUB + y, 2 * pairs, stride=back)
                wide[place, :] = wide[place, :] + contract(
                    second_w[g], flat[pl.ds(y, fold, stride=SUB), :]
                )
            for dc in (1, 0):
                start = pairs + (dev_g(dc) % 2) * SUB
                sends.append(pltpu.make_async_remote_copy(
                    src_ref=spread.at[h, pl.ds(start, SUB), g * SUB : (g + 1) * SUB, :],
                    dst_ref=landed.at[h, dc, :, g * SUB : (g + 1) * SUB, :],
                    send_sem=s1.at[h, dc, g], recv_sem=r1.at[h, dc, g],
                    device_id=(step_x(ix, way_of(g, groups, core), 1), dev_g(dc)),
                    device_id_type=MESH_ID,
                ))
                sends[-1].start()
        sends.append(copy(
            spread.at[h, pl.ds((1 - core) * SUB, SUB)], landed.at[h, 2], s5.at[h], r5.at[h], 0, 1
        ))
        sends[-1].start()
        return sends

    rows = SUB // PARTS
    nearby = {}

    def send_near(h, sends):
        for c in sends:
            c.wait_recv()
        for p in range(PARTS):
            at = slice(p * rows, (p + 1) * rows)
            own[h, at, 0] = spread[h, pl.ds(core * SUB + p * rows, rows)] + landed[h, 0, at]
            own[h, at, 1] = landed[h, 2, at] + landed[h, 1, at]
            nearby[h, p] = copy(
                own.at[h, at], near.at[h, at], s2.at[h, p], r2.at[h, p], 0, 2
            )
            nearby[h, p].start()

    first = receive_raw(0)
    for c in sm:
        c.wait_recv()
    block = small_out[ig]
    for d in range(1, ng):
        block = block + small_in[d - 1]
    small_sum[...] = block
    zx = []
    for d in range(1, nx):
        zx.append(copy(
            small_sum.at[0:SUB], zsum_in.at[d - 1], t3.at[d - 1], u3.at[d - 1], d, 0
        ))
        zx[-1].start()
    second = receive_raw(1)
    for c in zx:
        c.wait_recv()
    zpart = small_sum[0:SUB]
    for d in range(1, nx):
        zpart = zpart + zsum_in[d - 1]
    zx_out[0:SUB] = zpart
    zx_out[SUB:] = small_sum[SUB:]
    gathered = []
    for d in range(1, ng):
        gathered.append(copy(zx_out, zx_in.at[d - 1], t4.at[d - 1], u4.at[d - 1], 0, d))
        gathered[-1].start()
    send_near(0, first)
    send_near(1, second)
    pend += first + second + zx + gathered + list(nearby.values())

    parts = {}
    for h in range(2):
        for p in range(PARTS):
            nearby[h, p].wait_recv()
            for r in range(rows):
                at = p * rows + r
                pieces = split(own[h, at].reshape(2 * back, depth))
                pieces += split(near[h, at].reshape(2 * back, depth))
                total = mm(phi_y[...], jnp.concatenate(pieces, axis=0))
                keep[h, at] = total[:out_b]
                for k in range(3):
                    part_out[h, p, k, r] = total[(k + 1) * out_b : (k + 2) * out_b]
            for k, d in ((1, 4), (2, 5), (0, 1)):
                parts[h, p, k] = copy(
                    part_out.at[h, p, k], part_in.at[h, p, k], s3.at[h, p, k], r3.at[h, p, k], 0, d
                )
                parts[h, p, k].start()
    pend += list(parts.values())

    for c in fy:
        c.wait_recv()
    value = fy_out[...]
    for d in range(1, nx):
        value = value + fy_in[d - 1]
    out_y[...] = (value * (1.0 / math.sqrt(front * nx * depth)))[:, :RANK]
    for c in gathered:
        c.wait_recv()
    for c in sm:
        c.wait_send()
    for d in range(ng):
        block = zx_out[...] if d == 0 else zx_in[d - 1]
        small_out[dev_g(d)] = block
    scale_x = 1.0 / math.sqrt(back * ng * depth)
    scale_z = 1.0 / math.sqrt(front * nx * back * ng)
    for d in range(ng):
        out_x[d * per : (d + 1) * per, :] = small_out[d, SUB : SUB + per, :RANK] * scale_x
        out_z[d * kper : (d + 1) * kper, :] = small_out[d, 0:kper] * scale_z

    scale = 1.0 / math.sqrt(front * nx * back * ng * depth)
    count = rows * out_b
    for h in range(2):
        for p in range(PARTS):
            for k in range(3):
                parts[h, p, k].wait_recv()
            at = slice(p * rows, (p + 1) * rows)
            mine = (keep[h, at] + part_in[h, p, 1]).reshape(count, depth)
            other = (part_in[h, p, 0] + part_in[h, p, 2]).reshape(count, depth)
            high, low = split(jnp.concatenate([mine, other], axis=0))
            value = (mm(high, phi_z[h]) + mm(low, phi_z[h])) * scale
            for i in range(2):
                for which in range(2):
                    side = core if which == 0 else 1 - core
                    start = pl.multiple_of((i * pairs + side * SUB + p * rows) * out_b, SUB)
                    place = pl.ds(start, count)
                    piece = value[which * count : (which + 1) * count, i * LANES : (i + 1) * LANES]
                    out_core[place, :] = piece if h == 0 else out_core[place, :] + piece
    for c in pend:
        c.wait_send()


def publish(*refs):
    ready, out, sems = refs[:4], refs[4:8], refs[8]
    copies = [pltpu.make_async_copy(a, b, sems.at[i]) for i, (a, b) in enumerate(zip(ready, out))]
    for c in copies:
        c.start()
    for c in copies:
        c.wait()


def fused_body(nx, ng, thermal_field, generator_keys, slab_top_offset):
    front, back, depth = thermal_field.shape
    blk_a = TARGET_RANK // nx
    out_b = TARGET_RANK // ng
    f32 = jnp.float32
    bf16 = jnp.bfloat16
    vmem = pltpu.VMEM
    dma = pltpu.SemaphoreType.DMA
    groups = back // SUB
    rows = SUB // PARTS
    scratch = [
        pltpu.SMEM(generator_keys.shape, jnp.int32),
        vmem((front, back, depth), f32),
        dma((2,)),
        vmem((2, groups, front // 2, SUB, depth), f32),
        vmem((2, groups, front // 2, SUB, depth), f32),
        vmem((2, blk_a, back, depth), f32),
        vmem((2, 3, SUB, back, depth), f32),
        vmem((2, SUB, 2, back, depth), f32),
        vmem((2, SUB, 2, back, depth), f32),
        vmem((2, SUB, out_b, depth), f32),
        vmem((2, PARTS, 3, rows, out_b, depth), f32),
        vmem((2, PARTS, 3, rows, out_b, depth), f32),
        vmem((groups, 2 * blk_a, 2 * front), bf16),
        vmem((groups, 2 * blk_a, 2 * front), bf16),
        vmem((4 * out_b, 8 * back), bf16),
        vmem((2, depth, 2 * LANES), bf16),
        vmem((ng, 2 * SUB, LANES), f32),
        vmem((ng - 1, 2 * SUB, LANES), f32),
        vmem((2 * SUB, LANES), f32),
        vmem((nx - 1, SUB, LANES), f32),
        vmem((2 * SUB, LANES), f32),
        vmem((ng - 1, 2 * SUB, LANES), f32),
        vmem((back, LANES), f32),
        vmem((nx - 1, back, LANES), f32),
        dma((2, groups)), dma((2, groups)),
        dma((2,)), dma((2,)),
        dma((2, 2, groups)), dma((2, 2, groups)),
        dma((2, PARTS)), dma((2, PARTS)),
        dma((2, PARTS, 3)), dma((2, PARTS, 3)),
        dma((nx - 1,)), dma((nx - 1,)),
        dma((ng - 1,)), dma((ng - 1,)),
        dma((nx - 1,)), dma((nx - 1,)),
        dma((ng - 1,)), dma((ng - 1,)),
    ]
    whole = pl.BlockSpec(memory_space=pltpu.VMEM)
    far = pl.BlockSpec(memory_space=pltpu.HBM)
    shapes = (
        jax.ShapeDtypeStruct((front, RANK), f32),
        jax.ShapeDtypeStruct((back, RANK), f32),
        jax.ShapeDtypeStruct((RANK, depth), f32),
        jax.ShapeDtypeStruct((blk_a * out_b, depth), f32),
    )
    def stay(array):
        return pltpu.with_memory_space_constraint(array, pltpu.HBM)

    results = pl.pallas_call(
        functools.partial(kernel, (nx, ng, front, back, depth)),
        out_shape=shapes,
        in_specs=[far, pl.BlockSpec(memory_space=pltpu.SMEM), far],
        out_specs=(whole,) * 4,
        scratch_shapes=scratch,
        compiler_params=pltpu.CompilerParams(
            collective_id=0, has_side_effects=True, vmem_limit_bytes=40 * 2**20
        ),
    )(stay(generator_keys), slab_top_offset, stay(thermal_field))
    fx, fy, fz, core = pl.pallas_call(
        publish,
        out_shape=shapes,
        in_specs=[whole] * 4,
        out_specs=(far,) * 4,
        scratch_shapes=[dma((4,))],
        compiler_params=pltpu.CompilerParams(vmem_limit_bytes=2**20),
    )(*results)
    return fx, fy, fz.T, core.reshape(blk_a, out_b, depth)


def suits(nx, ng):
    return nx == 4 and ng == 8


def solution(mesh):
    nx, ng = mesh.shape["gx"], mesh.shape["gy"]
    chosen = functools.partial(fused_body, nx, ng) if suits(nx, ng) else body
    placed = (P("gx", "gy", None), P(), P())
    return jax.shard_map(
        chosen,
        mesh=mesh,
        in_specs=placed,
        out_specs=(P("gx", None), P("gy", None), P(), P("gx", "gy", None)),
        check_vma=False,
    )
```

time: 46 us -> 38.5 us (0.84)
  Pallas kernels: 40.7 us -> 36.7 us
  local copies, waits for them, and re-layouts: 3.67 us -> 0 us
    pallas_call x1, Pallas kernels: 40.7 us -> 35.9 us  [fused_body(): pl.pallas_call(functools.partial(kernel, (nx, ng, front, back, depth)), o...]
    unnamed x8 -> x0, local copies, waits for them, and re-layouts: 3.67 us -> none
    pallas_call x0 -> x1, Pallas kernels: none -> 0.76 us  [fused_body(): pl.pallas_call(publish, out_shape=shapes, in_specs=[whole] * 4, out_specs...]
where the time goes in v1:
time: 38.5 us; the launch traced here: 38 us
  Pallas kernels  36.7 us (95%)
  between operations  1.29 us (3%)
    pallas_call x1, Pallas kernels, fused_body(): pl.pallas_call(functools.partial(kernel, (nx, ng, front, back, depth)), o...  35.9 us

profile of v1, /device:TPU:0, one launch (start us, length us, event | category | flops | bytes accessed | tf_op | source)
XLA Modules:
  0.0 38.0 jit_solution(5214779970490101132)
XLA Ops:
  1.3 35.9 %shard_map.66 = (f32[48,64]{1,0:T(8,128)S(1)}, f32[24,64]{1,0:T(8,128)S(1)}, f32[64,128]{1,0:T(8,128)S(1)}, f32[512,128]{1,0:T(8,128)S(1)}) custom-call(s32[6]{0:T(128)} %keys_in.1, s32[1]{0:T(128)S(6)} %copy.7.top, f32[48,24,128]{2,1,0:T(8,128)} %field_in.1), custom_call_target="tpu_custom_call" | custom-call | tf_op jit(solution)/shard_map/pallas_call | solution.py:500
  37.2 0.8 %shard_map.67 = (f32[48,64]{1,0:T(8,128)}, f32[24,64]{1,0:T(8,128)}, f32[64,128]{1,0:T(8,128)}, f32[512,128]{1,0:T(8,128)}) custom-call(f32[48,64]{1,0:T(8,128)S(1)} %get-tuple-element.12.refs_0_, f32[24,64]{1,0:T(8,128)S(1)} %get-tuple-element.13.refs_1_, f32[64,128]{1,0:T(8,128)S(1)} %get-tuple-element.14.refs_2_, f32[512,128]{1,0:T(8,128)S(1)} %get-tuple-element.15.refs_3_), custom_call_target="tpu_custom_call" | custom-call | tf_op jit(solution)/shard_map/pallas_call | solution.py:510

commit v2 on v1

--- a/solution.py
+++ b/solution.py
@@ -112,9 +112,9 @@
     return index + bit - 2 * bit * ((index // bit) % 2)
 
 
-def way_of(group, groups, core):
+def way_of(group, groups, half):
     if 2 * group + 1 == groups:
-        return core
+        return half
     return 0 if 2 * group < groups else 1
 
 
@@ -199,7 +199,7 @@
             raws[h, g] = pltpu.make_async_remote_copy(
                 src_ref=raw_out.at[h, g], dst_ref=raw_in.at[h, g],
                 send_sem=s0.at[h, g], recv_sem=r0.at[h, g],
-                device_id=(step_x(ix, way_of(g, groups, core), 0), ig), device_id_type=MESH_ID,
+                device_id=(step_x(ix, way_of(g, groups, h), 0), ig), device_id_type=MESH_ID,
             )
             raws[h, g].start()
     pend = list(raws.values())
@@ -234,17 +234,12 @@
     for d in range(ng):
         small_out[d, 0:kper] = total_z[d * kper : (d + 1) * kper]
         small_out[d, SUB : SUB + per] = part_x[d * per : (d + 1) * per]
-    fy = []
-    for d in range(1, nx):
-        fy.append(copy(fy_out, fy_in.at[d - 1], t1.at[d - 1], u1.at[d - 1], d, 0))
-        fy[-1].start()
     sm = []
     for d in range(1, ng):
         sm.append(copy(
             small_out.at[dev_g(d)], small_in.at[d - 1], t2.at[d - 1], u2.at[d - 1], 0, d
         ))
         sm[-1].start()
-    pend += fy
 
     def weights(base, far_x):
         shape = (4 * pairs, 4 * fold)
@@ -259,10 +254,9 @@
         target = jnp.where(second, target + pairs, target)
         return signs(keys[3], cell, target).astype(jnp.bfloat16)
 
-    for g in range(groups):
-        way = way_of(g, groups, core)
-        first_w[g] = weights(x0, step_x(ix, way, 1))
-        second_w[g] = weights(step_x(ix, way, 0) * front, step_x(ix, way, 1))
+    for way in range(2):
+        first_w[way] = weights(x0, step_x(ix, way, 1))
+        second_w[way] = weights(step_x(ix, way, 0) * front, step_x(ix, way, 1))
 
     lower_row = iota((2 * pairs, depth), 1) < deep
 
@@ -278,7 +272,7 @@
             flat = raw_out.at[h, g].reshape(fold * SUB, depth)
             for y in range(SUB):
                 wide[pl.ds(g * SUB + y, 2 * pairs, stride=back), :] = contract(
-                    first_w[g], flat[pl.ds(y, fold, stride=SUB), :]
+                    first_w[way_of(g, groups, h)], flat[pl.ds(y, fold, stride=SUB), :]
                 )
 
     shape = (4 * out_b, 4 * back)
@@ -301,40 +295,46 @@
     for h in range(2):
         phi_z[h] = jnp.where(same, signs(keys[5], row + h * deep, col), 0.0).astype(jnp.bfloat16)
 
+    rows = SUB // PARTS
+
     def receive_raw(h):
         wide = spread.at[h].reshape(2 * pairs * back, depth)
-        sends = []
+        sends = [[] for _ in range(PARTS)]
         for g in order:
             raws[h, g].wait_recv()
             flat = raw_in.at[h, g].reshape(fold * SUB, depth)
             for y in range(SUB):
                 place = pl.ds(g * SUB + y, 2 * pairs, stride=back)
                 wide[place, :] = wide[place, :] + contract(
-                    second_w[g], flat[pl.ds(y, fold, stride=SUB), :]
+                    second_w[way_of(g, groups, h)], flat[pl.ds(y, fold, stride=SUB), :]
                 )
-            for dc in (1, 0):
-                start = pairs + (dev_g(dc) % 2) * SUB
-                sends.append(pltpu.make_async_remote_copy(
-                    src_ref=spread.at[h, pl.ds(start, SUB), g * SUB : (g + 1) * SUB, :],
-                    dst_ref=landed.at[h, dc, :, g * SUB : (g + 1) * SUB, :],
-                    send_sem=s1.at[h, dc, g], recv_sem=r1.at[h, dc, g],
-                    device_id=(step_x(ix, way_of(g, groups, core), 1), dev_g(dc)),
-                    device_id_type=MESH_ID,
-                ))
-                sends[-1].start()
-        sends.append(copy(
-            spread.at[h, pl.ds((1 - core) * SUB, SUB)], landed.at[h, 2], s5.at[h], r5.at[h], 0, 1
-        ))
-        sends[-1].start()
+            for p in range(PARTS):
+                for dc in (1, 0):
+                    start = pairs + (dev_g(dc) % 2) * SUB + p * rows
+                    ys = slice(g * SUB, (g + 1) * SUB)
+                    sends[p].append(pltpu.make_async_remote_copy(
+                        src_ref=spread.at[h, pl.ds(start, rows), ys, :],
+                        dst_ref=landed.at[h, dc, p * rows : (p + 1) * rows, ys, :],
+                        send_sem=s1.at[h, p, dc, g], recv_sem=r1.at[h, p, dc, g],
+                        device_id=(step_x(ix, way_of(g, groups, h), 1), dev_g(dc)),
+                        device_id_type=MESH_ID,
+                    ))
+                    sends[p][-1].start()
+        for p in range(PARTS):
+            sends[p].append(copy(
+                spread.at[h, pl.ds((1 - core) * SUB + p * rows, rows)],
+                landed.at[h, 2, p * rows : (p + 1) * rows],
+                s5.at[h, p], r5.at[h, p], 0, 1,
+            ))
+            sends[p][-1].start()
         return sends
 
-    rows = SUB // PARTS
     nearby = {}
 
     def send_near(h, sends):
-        for c in sends:
-            c.wait_recv()
         for p in range(PARTS):
+            for c in sends[p]:
+                c.wait_recv()
             at = slice(p * rows, (p + 1) * rows)
             own[h, at, 0] = spread[h, pl.ds(core * SUB + p * rows, rows)] + landed[h, 0, at]
             own[h, at, 1] = landed[h, 2, at] + landed[h, 1, at]
@@ -357,6 +357,11 @@
         ))
         zx[-1].start()
     second = receive_raw(1)
+    fy = []
+    for d in range(1, nx):
+        fy.append(copy(fy_out, fy_in.at[d - 1], t1.at[d - 1], u1.at[d - 1], d, 0))
+        fy[-1].start()
+    pend += fy
     for c in zx:
         c.wait_recv()
     zpart = small_sum[0:SUB]
@@ -370,7 +375,7 @@
         gathered[-1].start()
     send_near(0, first)
     send_near(1, second)
-    pend += first + second + zx + gathered + list(nearby.values())
+    pend += sum(first + second, []) + zx + gathered + list(nearby.values())
 
     parts = {}
     for h in range(2):
@@ -464,8 +469,8 @@
         vmem((2, SUB, out_b, depth), f32),
         vmem((2, PARTS, 3, rows, out_b, depth), f32),
         vmem((2, PARTS, 3, rows, out_b, depth), f32),
-        vmem((groups, 2 * blk_a, 2 * front), bf16),
-        vmem((groups, 2 * blk_a, 2 * front), bf16),
+        vmem((2, 2 * blk_a, 2 * front), bf16),
+        vmem((2, 2 * blk_a, 2 * front), bf16),
         vmem((4 * out_b, 8 * back), bf16),
         vmem((2, depth, 2 * LANES), bf16),
         vmem((ng, 2 * SUB, LANES), f32),
@@ -477,8 +482,8 @@
         vmem((back, LANES), f32),
         vmem((nx - 1, back, LANES), f32),
         dma((2, groups)), dma((2, groups)),
-        dma((2,)), dma((2,)),
-        dma((2, 2, groups)), dma((2, 2, groups)),
+        dma((2, PARTS)), dma((2, PARTS)),
+        dma((2, PARTS, 2, groups)), dma((2, PARTS, 2, groups)),
         dma((2, PARTS)), dma((2, PARTS)),
         dma((2, PARTS, 3)), dma((2, PARTS, 3)),
         dma((nx - 1,)), dma((nx - 1,)),

time: 38.5 us -> 38.5 us (level)
  no operation moved by 1% of the time
where the time goes in v2:
time: 38.5 us; the launch traced here: 38 us
  Pallas kernels  36.7 us (95%)
  between operations  1.29 us (3%)
    pallas_call x1, Pallas kernels, fused_body(): pl.pallas_call(functools.partial(kernel, (nx, ng, front, back, depth)), o...  36 us

profile of v2, /device:TPU:0, one launch (start us, length us, event | category | flops | bytes accessed | tf_op | source)
XLA Modules:
  0.0 38.0 jit_solution(13978877778502765019)
XLA Ops:
  1.3 36.0 %shard_map.66 = (f32[48,64]{1,0:T(8,128)S(1)}, f32[24,64]{1,0:T(8,128)S(1)}, f32[64,128]{1,0:T(8,128)S(1)}, f32[512,128]{1,0:T(8,128)S(1)}) custom-call(s32[6]{0:T(128)} %keys_in.1, s32[1]{0:T(128)S(6)} %copy.7.top, f32[48,24,128]{2,1,0:T(8,128)} %field_in.1), custom_call_target="tpu_custom_call" | custom-call | tf_op jit(solution)/shard_map/pallas_call | solution.py:505
  37.2 0.8 %shard_map.67 = (f32[48,64]{1,0:T(8,128)}, f32[24,64]{1,0:T(8,128)}, f32[64,128]{1,0:T(8,128)}, f32[512,128]{1,0:T(8,128)}) custom-call(f32[48,64]{1,0:T(8,128)S(1)} %get-tuple-element.12.refs_0_, f32[24,64]{1,0:T(8,128)S(1)} %get-tuple-element.13.refs_1_, f32[64,128]{1,0:T(8,128)S(1)} %get-tuple-element.14.refs_2_, f32[512,128]{1,0:T(8,128)S(1)} %get-tuple-element.15.refs_3_), custom_call_target="tpu_custom_call" | custom-call | tf_op jit(solution)/shard_map/pallas_call | solution.py:515

commit v3 on v2

--- a/solution.py
+++ b/solution.py
@@ -129,10 +129,10 @@
     dims,
     keys_in, top, field_in,
     out_x, out_y, out_z, out_core,
-    keys, field, load_sem, raw_out, raw_in, spread, landed, own, near, keep, part_out, part_in,
-    first_w, second_w, phi_y, phi_z,
+    keys, field, load_sem, raw_out, raw_in, spread, landed, own, near, keep, edge_out, part_out, part_in,
+    first_w, second_w, phi_y, phi_edge, phi_z,
     small_out, small_in, small_sum, zsum_in, zx_out, zx_in, fy_out, fy_in,
-    s0, r0, s5, r5, s1, r1, s2, r2, s3, r3, t1, u1, t2, u2, t3, u3, t4, u4,
+    s0, r0, s5, r5, s1, r1, s2, r2, s3, r3, s6, t1, u1, t2, u2, t3, u3, t4, u4,
 ):
     nx, ng, front, back, depth = dims
     nz = ng // 2
@@ -142,6 +142,7 @@
     ix = lax.axis_index("gx")
     ig = lax.axis_index("gy")
     iz, core = ig // 2, ig % 2
+    inner = ((iz + 1) // 2) % 2
 
     def dev_x(d):
         r = ix
@@ -185,7 +186,7 @@
     lower = iota((fold, SUB, depth), 2) < deep
     load.wait()
     for h in range(2):
-        for g in range(groups):
+        for g in order:
             here = field[0:fold, g * SUB : (g + 1) * SUB, :]
             there = field[fold:front, g * SUB : (g + 1) * SUB, :]
             if h == 0:
@@ -275,18 +276,30 @@
                     first_w[way_of(g, groups, h)], flat[pl.ds(y, fold, stride=SUB), :]
                 )
 
-    shape = (4 * out_b, 4 * back)
+    shape = (6 * out_b, 4 * back)
     row = iota(shape, 0)
     col = iota(shape, 1)
     col = jnp.where(col >= 2 * back, col - 2 * back, col)
     target = row
-    for k, d in enumerate((0, 1, 4, 5)):
+    for k, d in enumerate((4, 5, 6, 7, 0, 1)):
         target = jnp.where(row >= k * out_b, row + (dev_g(d) - k) * out_b, target)
     for src in range(2):
         cell = jnp.where(col >= back, dev_g(2 * src + 1) * back - back, dev_g(2 * src) * back) + col
         phi_y[:, src * 4 * back : (src + 1) * 4 * back] = signs(keys[4], cell, target).astype(
             jnp.bfloat16
         )
+        if src == 0:
+            row = row[: 2 * out_b]
+            here = ig + (dev_g(2) - ig) * inner
+            there = dev_g(1) + (dev_g(3) - dev_g(1)) * inner
+            target_edge = row + jnp.where(row >= out_b, there - 1, here) * out_b
+            phi_edge[...] = signs(keys[4], cell[: 2 * out_b], target_edge).astype(jnp.bfloat16)
+
+    @pl.when(inner == 1)
+    def _():
+        for h in range(2):
+            part_in[h, :, 3:5] = jnp.zeros((PARTS, 2, SUB // PARTS, out_b, depth), jnp.float32)
+
     row = iota((depth, 2 * LANES), 0)
     col = iota((depth, 2 * LANES), 1)
     same = (row >= deep) == (col >= LANES)
@@ -296,6 +309,20 @@
         phi_z[h] = jnp.where(same, signs(keys[5], row + h * deep, col), 0.0).astype(jnp.bfloat16)
 
     rows = SUB // PARTS
+    zx = []
+
+    def sum_small():
+        for c in sm:
+            c.wait_recv()
+        block = small_out[ig]
+        for d in range(1, ng):
+            block = block + small_in[d - 1]
+        small_sum[...] = block
+        for d in range(1, nx):
+            zx.append(copy(
+                small_sum.at[0:SUB], zsum_in.at[d - 1], t3.at[d - 1], u3.at[d - 1], d, 0
+            ))
+            zx[-1].start()
 
     def receive_raw(h):
         wide = spread.at[h].reshape(2 * pairs * back, depth)
@@ -304,8 +331,8 @@
             raws[h, g].wait_recv()
             flat = raw_in.at[h, g].reshape(fold * SUB, depth)
             for y in range(SUB):
-                place = pl.ds(g * SUB + y, 2 * pairs, stride=back)
-                wide[place, :] = wide[place, :] + contract(
+                strip = pl.ds(g * SUB + y, 2 * pairs, stride=back)
+                wide[strip, :] = wide[strip, :] + contract(
                     second_w[way_of(g, groups, h)], flat[pl.ds(y, fold, stride=SUB), :]
                 )
             for p in range(PARTS):
@@ -330,38 +357,56 @@
         return sends
 
     nearby = {}
-
-    def send_near(h, sends):
-        for p in range(PARTS):
-            for c in sends[p]:
-                c.wait_recv()
-            at = slice(p * rows, (p + 1) * rows)
-            own[h, at, 0] = spread[h, pl.ds(core * SUB + p * rows, rows)] + landed[h, 0, at]
-            own[h, at, 1] = landed[h, 2, at] + landed[h, 1, at]
-            nearby[h, p] = copy(
-                own.at[h, at], near.at[h, at], s2.at[h, p], r2.at[h, p], 0, 2
+    edges = {}
+    share = {}
+
+    def send_near(h, p, sends):
+        for c in sends[p]:
+            c.wait_recv()
+        at = slice(p * rows, (p + 1) * rows)
+        own[h, at, 0] = spread[h, pl.ds(core * SUB + p * rows, rows)] + landed[h, 0, at]
+        own[h, at, 1] = landed[h, 2, at] + landed[h, 1, at]
+        nearby[h, p] = copy(own.at[h, at], near.at[h, at], s2.at[h, p], r2.at[h, p], 0, 2)
+
+        @pl.when(inner == 0)
+        def _():
+            nearby[h, p].start()
+
+        for r in range(rows):
+            pieces = split(own[h, p * rows + r].reshape(2 * back, depth))
+            total = mm(phi_edge[...], jnp.concatenate(pieces, axis=0))
+            edge_out[h, p, 0, r] = total[:out_b]
+            edge_out[h, p, 1, r] = total[out_b:]
+        for k in range(2):
+            edges[h, p, k] = copy(
+                edge_out.at[h, p, k], part_in.at[h, p, 3 + k],
+                s3.at[h, p, 3 + k], r3.at[h, p, 3 + k], 0, 2 + k,
             )
-            nearby[h, p].start()
+        share[h, p, 0] = copy(
+            edge_out.at[h, p, 1], part_in.at[h, p, 0], s3.at[h, p, 0], r3.at[h, p, 0], 0, 1
+        )
+
+        @pl.when(inner == 1)
+        def _():
+            edges[h, p, 0].start()
+            edges[h, p, 1].start()
+
+        @pl.when(inner == 0)
+        def _():
+            keep[h, at] = edge_out[h, p, 0]
+            share[h, p, 0].start()
+
 
     first = receive_raw(0)
-    for c in sm:
-        c.wait_recv()
-    block = small_out[ig]
-    for d in range(1, ng):
-        block = block + small_in[d - 1]
-    small_sum[...] = block
-    zx = []
-    for d in range(1, nx):
-        zx.append(copy(
-            small_sum.at[0:SUB], zsum_in.at[d - 1], t3.at[d - 1], u3.at[d - 1], d, 0
-        ))
-        zx[-1].start()
+    sum_small()
     second = receive_raw(1)
     fy = []
     for d in range(1, nx):
         fy.append(copy(fy_out, fy_in.at[d - 1], t1.at[d - 1], u1.at[d - 1], d, 0))
         fy[-1].start()
     pend += fy
+    send_near(0, 0, first)
+    send_near(0, 1, first)
     for c in zx:
         c.wait_recv()
     zpart = small_sum[0:SUB]
@@ -373,28 +418,36 @@
     for d in range(1, ng):
         gathered.append(copy(zx_out, zx_in.at[d - 1], t4.at[d - 1], u4.at[d - 1], 0, d))
         gathered[-1].start()
-    send_near(0, first)
-    send_near(1, second)
-    pend += sum(first + second, []) + zx + gathered + list(nearby.values())
+    send_near(1, 0, second)
+    send_near(1, 1, second)
+    pend += sum(first + second, []) + zx + gathered
 
     parts = {}
+    ways = ((0, 4, 1), (1, 5, 2), (2, 6, 1), (3, 7, 2), (4, 1, 0))
     for h in range(2):
         for p in range(PARTS):
-            nearby[h, p].wait_recv()
-            for r in range(rows):
-                at = p * rows + r
-                pieces = split(own[h, at].reshape(2 * back, depth))
-                pieces += split(near[h, at].reshape(2 * back, depth))
-                total = mm(phi_y[...], jnp.concatenate(pieces, axis=0))
-                keep[h, at] = total[:out_b]
-                for k in range(3):
-                    part_out[h, p, k, r] = total[(k + 1) * out_b : (k + 2) * out_b]
-            for k, d in ((1, 4), (2, 5), (0, 1)):
+            for k, d, slot in ways:
                 parts[h, p, k] = copy(
-                    part_out.at[h, p, k], part_in.at[h, p, k], s3.at[h, p, k], r3.at[h, p, k], 0, d
+                    part_out.at[h, p, k], part_in.at[h, p, slot],
+                    s6.at[h, p, k], r3.at[h, p, slot], 0, d,
                 )
-                parts[h, p, k].start()
-    pend += list(parts.values())
+
+    @pl.when(inner == 1)
+    def _():
+        for h in range(2):
+            for p in range(PARTS):
+                nearby[h, p].wait_recv()
+                for r in range(rows):
+                    at = p * rows + r
+                    pieces = split(own[h, at].reshape(2 * back, depth))
+                    pieces += split(near[h, at].reshape(2 * back, depth))
+                    total = mm(phi_y[...], jnp.concatenate(pieces, axis=0))
+                    keep[h, at] = total[4 * out_b : 5 * out_b]
+                    for k in range(5):
+                        first = (k if k < 4 else 5) * out_b
+                        part_out[h, p, k, r] = total[first : first + out_b]
+                for k in range(5):
+                    parts[h, p, k].start()
 
     for c in fy:
         c.wait_recv()
@@ -419,11 +472,19 @@
     count = rows * out_b
     for h in range(2):
         for p in range(PARTS):
-            for k in range(3):
-                parts[h, p, k].wait_recv()
+            @pl.when(inner == 0)
+            def _():
+                edges[h, p, 0].wait_recv()
+                edges[h, p, 1].wait_recv()
+
+            share[h, p, 0].wait_recv()
+            parts[h, p, 0].wait_recv()
+            parts[h, p, 1].wait_recv()
             at = slice(p * rows, (p + 1) * rows)
-            mine = (keep[h, at] + part_in[h, p, 1]).reshape(count, depth)
-            other = (part_in[h, p, 0] + part_in[h, p, 2]).reshape(count, depth)
+            mine = keep[h, at] + part_in[h, p, 3] + part_in[h, p, 1]
+            other = part_in[h, p, 0] + part_in[h, p, 4] + part_in[h, p, 2]
+            mine = mine.reshape(count, depth)
+            other = other.reshape(count, depth)
             high, low = split(jnp.concatenate([mine, other], axis=0))
             value = (mm(high, phi_z[h]) + mm(low, phi_z[h])) * scale
             for i in range(2):
@@ -435,6 +496,16 @@
                     out_core[place, :] = piece if h == 0 else out_core[place, :] + piece
     for c in pend:
         c.wait_send()
+
+    @pl.when(inner == 0)
+    def _():
+        for c in list(nearby.values()) + list(share.values()):
+            c.wait_send()
+
+    @pl.when(inner == 1)
+    def _():
+        for c in list(edges.values()) + list(parts.values()):
+            c.wait_send()
 
 
 def publish(*refs):
@@ -467,11 +538,13 @@
         vmem((2, SUB, 2, back, depth), f32),
         vmem((2, SUB, 2, back, depth), f32),
         vmem((2, SUB, out_b, depth), f32),
-        vmem((2, PARTS, 3, rows, out_b, depth), f32),
-        vmem((2, PARTS, 3, rows, out_b, depth), f32),
+        vmem((2, PARTS, 2, rows, out_b, depth), f32),
+        vmem((2, PARTS, 5, rows, out_b, depth), f32),
+        vmem((2, PARTS, 5, rows, out_b, depth), f32),
         vmem((2, 2 * blk_a, 2 * front), bf16),
         vmem((2, 2 * blk_a, 2 * front), bf16),
-        vmem((4 * out_b, 8 * back), bf16),
+        vmem((6 * out_b, 8 * back), bf16),
+        vmem((2 * out_b, 4 * back), bf16),
         vmem((2, depth, 2 * LANES), bf16),
         vmem((ng, 2 * SUB, LANES), f32),
         vmem((ng - 1, 2 * SUB, LANES), f32),
@@ -485,7 +558,7 @@
         dma((2, PARTS)), dma((2, PARTS)),
         dma((2, PARTS, 2, groups)), dma((2, PARTS, 2, groups)),
         dma((2, PARTS)), dma((2, PARTS)),
-        dma((2, PARTS, 3)), dma((2, PARTS, 3)),
+        dma((2, PARTS, 5)), dma((2, PARTS, 5)), dma((2, PARTS, 5)),
         dma((nx - 1,)), dma((nx - 1,)),
         dma((ng - 1,)), dma((ng - 1,)),
         dma((nx - 1,)), dma((nx - 1,)),

time: 38.5 us -> 36.5 us (0.948)
  Pallas kernels: 36.7 us -> 35.1 us
    pallas_call x1, Pallas kernels: 36 us -> 34.3 us  [fused_body(): pl.pallas_call(functools.partial(kernel, (nx, ng, front, back, depth)), o...]
where the time goes in v3:
time: 36.5 us; the launch traced here: 36.3 us
  Pallas kernels  35.1 us (96%)
  between operations  1.29 us (4%)
    pallas_call x1, Pallas kernels, fused_body(): pl.pallas_call(functools.partial(kernel, (nx, ng, front, back, depth)), o...  34.3 us
    pallas_call x1, Pallas kernels, fused_body(): pl.pallas_call(publish, out_shape=shapes, in_specs=[whole] * 4, out_specs...  0.76 us

profile of v3, /device:TPU:0, one launch (start us, length us, event | category | flops | bytes accessed | tf_op | source)
XLA Modules:
  0.0 36.3 jit_solution(4866649235441781613)
XLA Ops:
  1.3 34.3 %shard_map.66 = (f32[48,64]{1,0:T(8,128)S(1)}, f32[24,64]{1,0:T(8,128)S(1)}, f32[64,128]{1,0:T(8,128)S(1)}, f32[512,128]{1,0:T(8,128)S(1)}) custom-call(s32[6]{0:T(128)} %keys_in.1, s32[1]{0:T(128)S(6)} %copy.7.top, f32[48,24,128]{2,1,0:T(8,128)} %field_in.1), custom_call_target="tpu_custom_call" | custom-call | tf_op jit(solution)/shard_map/pallas_call | solution.py:578
  35.6 0.8 %shard_map.67 = (f32[48,64]{1,0:T(8,128)}, f32[24,64]{1,0:T(8,128)}, f32[64,128]{1,0:T(8,128)}, f32[512,128]{1,0:T(8,128)}) custom-call(f32[48,64]{1,0:T(8,128)S(1)} %get-tuple-element.12.refs_0_, f32[24,64]{1,0:T(8,128)S(1)} %get-tuple-element.13.refs_1_, f32[64,128]{1,0:T(8,128)S(1)} %get-tuple-element.14.refs_2_, f32[512,128]{1,0:T(8,128)S(1)} %get-tuple-element.15.refs_3_), custom_call_target="tpu_custom_call" | custom-call | tf_op jit(solution)/shard_map/pallas_call | solution.py:588

commit v4 on v3

--- a/solution.py
+++ b/solution.py
@@ -372,6 +372,8 @@
         def _():
             nearby[h, p].start()
 
+    def send_edges(h, p):
+        at = slice(p * rows, (p + 1) * rows)
         for r in range(rows):
             pieces = split(own[h, p * rows + r].reshape(2 * back, depth))
             total = mm(phi_edge[...], jnp.concatenate(pieces, axis=0))
@@ -405,8 +407,10 @@
         fy.append(copy(fy_out, fy_in.at[d - 1], t1.at[d - 1], u1.at[d - 1], d, 0))
         fy[-1].start()
     pend += fy
-    send_near(0, 0, first)
-    send_near(0, 1, first)
+    for p in range(PARTS):
+        send_near(0, p, first)
+    for p in range(PARTS):
+        send_edges(0, p)
     for c in zx:
         c.wait_recv()
     zpart = small_sum[0:SUB]
@@ -418,8 +422,10 @@
     for d in range(1, ng):
         gathered.append(copy(zx_out, zx_in.at[d - 1], t4.at[d - 1], u4.at[d - 1], 0, d))
         gathered[-1].start()
-    send_near(1, 0, second)
-    send_near(1, 1, second)
+    for p in range(PARTS):
+        send_near(1, p, second)
+    for p in range(PARTS):
+        send_edges(1, p)
     pend += sum(first + second, []) + zx + gathered
 
     parts = {}
@@ -468,10 +474,31 @@
         out_x[d * per : (d + 1) * per, :] = small_out[d, SUB : SUB + per, :RANK] * scale_x
         out_z[d * kper : (d + 1) * kper, :] = small_out[d, 0:kper] * scale_z
 
+    for c in pend:
+        c.wait_send()
+
+    @pl.when(inner == 0)
+    def _():
+        for c in list(nearby.values()) + list(share.values()):
+            c.wait_send()
+
+    @pl.when(inner == 1)
+    def _():
+        for c in edges.values():
+            c.wait_send()
+
     scale = 1.0 / math.sqrt(front * nx * back * ng * depth)
     count = rows * out_b
     for h in range(2):
         for p in range(PARTS):
+            if h or p:
+                before = (h, p - 1) if p else (h - 1, PARTS - 1)
+
+                @pl.when(inner == 1)
+                def _():
+                    for k in range(5):
+                        parts[before + (k,)].wait_send()
+
             @pl.when(inner == 0)
             def _():
                 edges[h, p, 0].wait_recv()
@@ -494,18 +521,10 @@
                     place = pl.ds(start, count)
                     piece = value[which * count : (which + 1) * count, i * LANES : (i + 1) * LANES]
                     out_core[place, :] = piece if h == 0 else out_core[place, :] + piece
-    for c in pend:
-        c.wait_send()
-
-    @pl.when(inner == 0)
-    def _():
-        for c in list(nearby.values()) + list(share.values()):
-            c.wait_send()
-
     @pl.when(inner == 1)
     def _():
-        for c in list(edges.values()) + list(parts.values()):
-            c.wait_send()
+        for k in range(5):
+            parts[1, PARTS - 1, k].wait_send()
 
 
 def publish(*refs):

time: 36.5 us -> 36.4 us (level)
  no operation moved by 1% of the time
where the time goes in v4:
time: 36.4 us; the launch traced here: 36.2 us
  Pallas kernels  35 us (96%)
  between operations  1.29 us (4%)
    pallas_call x1, Pallas kernels, fused_body(): pl.pallas_call(functools.partial(kernel, (nx, ng, front, back, depth)), o...  34.2 us
    pallas_call x1, Pallas kernels, fused_body(): pl.pallas_call(publish, out_shape=shapes, in_specs=[whole] * 4, out_specs...  0.76 us

profile of v4, /device:TPU:0, one launch (start us, length us, event | category | flops | bytes accessed | tf_op | source)
XLA Modules:
  0.0 36.2 jit_solution(6988132530364721903)
XLA Ops:
  1.3 34.2 %shard_map.66 = (f32[48,64]{1,0:T(8,128)S(1)}, f32[24,64]{1,0:T(8,128)S(1)}, f32[64,128]{1,0:T(8,128)S(1)}, f32[512,128]{1,0:T(8,128)S(1)}) custom-call(s32[6]{0:T(128)} %keys_in.1, s32[1]{0:T(128)S(6)} %copy.7.top, f32[48,24,128]{2,1,0:T(8,128)} %field_in.1), custom_call_target="tpu_custom_call" | custom-call | tf_op jit(solution)/shard_map/pallas_call | solution.py:597
  35.5 0.8 %shard_map.67 = (f32[48,64]{1,0:T(8,128)}, f32[24,64]{1,0:T(8,128)}, f32[64,128]{1,0:T(8,128)}, f32[512,128]{1,0:T(8,128)}) custom-call(f32[48,64]{1,0:T(8,128)S(1)} %get-tuple-element.12.refs_0_, f32[24,64]{1,0:T(8,128)S(1)} %get-tuple-element.13.refs_1_, f32[64,128]{1,0:T(8,128)S(1)} %get-tuple-element.14.refs_2_, f32[512,128]{1,0:T(8,128)S(1)} %get-tuple-element.15.refs_3_), custom_call_target="tpu_custom_call" | custom-call | tf_op jit(solution)/shard_map/pallas_call | solution.py:607

commit v5 on v4

--- a/solution.py
+++ b/solution.py
@@ -402,11 +402,6 @@
     first = receive_raw(0)
     sum_small()
     second = receive_raw(1)
-    fy = []
-    for d in range(1, nx):
-        fy.append(copy(fy_out, fy_in.at[d - 1], t1.at[d - 1], u1.at[d - 1], d, 0))
-        fy[-1].start()
-    pend += fy
     for p in range(PARTS):
         send_near(0, p, first)
     for p in range(PARTS):
@@ -426,6 +421,11 @@
         send_near(1, p, second)
     for p in range(PARTS):
         send_edges(1, p)
+    fy = []
+    for d in range(1, nx):
+        fy.append(copy(fy_out, fy_in.at[d - 1], t1.at[d - 1], u1.at[d - 1], d, 0))
+        fy[-1].start()
+    pend += fy
     pend += sum(first + second, []) + zx + gathered
 
     parts = {}

time: 36.4 us -> 36.4 us (level)
  no operation moved by 1% of the time
where the time goes in v5:
time: 36.4 us; the launch traced here: 36.2 us
  Pallas kernels  35 us (96%)
  between operations  1.29 us (4%)
    pallas_call x1, Pallas kernels, fused_body(): pl.pallas_call(functools.partial(kernel, (nx, ng, front, back, depth)), o...  34.2 us
    pallas_call x1, Pallas kernels, fused_body(): pl.pallas_call(publish, out_shape=shapes, in_specs=[whole] * 4, out_specs...  0.76 us

profile of v5, /device:TPU:0, one launch (start us, length us, event | category | flops | bytes accessed | tf_op | source)
XLA Modules:
  0.0 36.2 jit_solution(2427624029376018287)
XLA Ops:
  1.3 34.2 %shard_map.66 = (f32[48,64]{1,0:T(8,128)S(1)}, f32[24,64]{1,0:T(8,128)S(1)}, f32[64,128]{1,0:T(8,128)S(1)}, f32[512,128]{1,0:T(8,128)S(1)}) custom-call(s32[6]{0:T(128)} %keys_in.1, s32[1]{0:T(128)S(6)} %copy.7.top, f32[48,24,128]{2,1,0:T(8,128)} %field_in.1), custom_call_target="tpu_custom_call" | custom-call | tf_op jit(solution)/shard_map/pallas_call | solution.py:597
  35.5 0.8 %shard_map.67 = (f32[48,64]{1,0:T(8,128)}, f32[24,64]{1,0:T(8,128)}, f32[64,128]{1,0:T(8,128)}, f32[512,128]{1,0:T(8,128)}) custom-call(f32[48,64]{1,0:T(8,128)S(1)} %get-tuple-element.12.refs_0_, f32[24,64]{1,0:T(8,128)S(1)} %get-tuple-element.13.refs_1_, f32[64,128]{1,0:T(8,128)S(1)} %get-tuple-element.14.refs_2_, f32[512,128]{1,0:T(8,128)S(1)} %get-tuple-element.15.refs_3_), custom_call_target="tpu_custom_call" | custom-call | tf_op jit(solution)/shard_map/pallas_call | solution.py:607
